TPU v7x, 512 devices: a whole 4x8x8 slice. The times are simulated.
512 devices in a mesh: dp: 16 (over z, core), mp: 32 (over y, x).
Axes of the slice: x: 4, y: 8, z: 8, core: 2. Of those that a mesh axis runs over, the one named last changes fastest.
Arguments:
- activations: bfloat16 [32768, 8192], P('dp', 'mp'), as said below
- output_grads: bfloat16 [32768, 28672], P('dp', 'mp'), as said below
- probe_matrix: bfloat16 [28672, 128], P('mp'), may hold values from -6 to 6
Outputs:
- basis: float32 [8192, 128], P('mp')
- projection: float32 [128, 28672], P(None, 'mp')
Inputs may be any that keep to these rules, and one draw needn't show every extreme that they name: `activations`: finite real values of order one. `output_grads`: finite real values of order one.
All inputs are finite; a program needn't handle non-finite values.
Results may differ from a plain program's by a relative error of at most 0.035.
Values may be sent and summed in bfloat16 or wider, within the bound.
No kernel may reach another device: no remote copies, remote signals or barrier semaphores. Data moves between devices by JAX's collectives and lax.ppermute only.
A program may use at most 64 MiB of HBM per device.

v0:
```python
import jax
import jax.numpy as jnp
from jax import lax
from jax.sharding import PartitionSpec as P

H = 8192


def contract_rows(left, right):
    return lax.dot_general(
        left, right, (((0,), (0,)), ((), ())), preferred_element_type=jnp.float32
    )


def token_total(partial_value):
    return lax.psum(partial_value.astype(jnp.bfloat16), "mp")


def gram_of(matrix):
    return lax.dot_general(
        matrix,
        matrix,
        (((0,), (0,)), ((), ())),
        precision=lax.Precision.HIGHEST,
        preferred_element_type=jnp.float32,
    )


def solve_rows(factor, matrix):
    return lax.linalg.triangular_solve(
        factor, matrix, left_side=False, lower=True, transpose_a=True
    )


def orthonormalize(partial_value):
    summed = lax.psum(partial_value, "dp")
    gram_matrix = lax.psum(gram_of(summed), "mp")
    factor = jnp.linalg.cholesky(gram_matrix)
    return solve_rows(factor, summed)


def on_device(activations, output_grads, probe_matrix):
    probe_rows = token_total(
        jnp.dot(output_grads, probe_matrix, preferred_element_type=jnp.float32)
    )
    first_basis = orthonormalize(contract_rows(activations, probe_rows))
    token_rows = token_total(
        jnp.dot(activations, first_basis.astype(jnp.bfloat16), preferred_element_type=jnp.float32)
    )
    second_basis = orthonormalize(contract_rows(output_grads, token_rows))
    unit_rows = token_total(
        jnp.dot(output_grads, second_basis.astype(jnp.bfloat16), preferred_element_type=jnp.float32)
    )
    third_basis = orthonormalize(contract_rows(activations, unit_rows))
    last_rows = token_total(
        jnp.dot(activations, third_basis.astype(jnp.bfloat16), preferred_element_type=jnp.float32)
    )
    projected = contract_rows(last_rows, output_grads)
    projection = lax.psum(projected, "dp")
    basis = third_basis * jnp.sqrt(jnp.float32(H))
    return (basis, projection)


def solution(mesh):
    in_specs = (P("dp", "mp"), P("dp", "mp"), P("mp", None))
    out_specs = (P("mp", None), P(None, "mp"))
    return jax.shard_map(
        on_device, mesh=mesh, in_specs=in_specs, out_specs=out_specs, check_vma=False
    )
```

profile of v0, /device:TPU:1, one launch (start us, length us, event | category | flops | bytes accessed | tf_op | source)
XLA Modules:
  0.0 1659.9 jit_solution(11712549844243807659)
XLA Ops:
  7.2 4.1 convolution_convert_fusion.1
  11.4 159.3 %all-reduce.12.cloned.1.call-done = bf16[2048,128]{1,0:T(8,128)(2,1)} async-done(((bf16[2048,128]{1,0:T(8,128)(2,1)}), bf16[2048,128]{1,0:T(8,128)(2,1)}) %all-reduce.12.cloned.1.call-update) | async-done | bytes 524304 | tf_op jit(solution)/shard_map/psum | solution.py:16
  170.7 2.0 convolution_bitcast_fusion.4
  172.8 116.4 %all-reduce.14.cloned.1.call-done = f32[256,128]{0,1:T(8,128)} async-done(((f32[256,128]{0,1:T(8,128)}), f32[256,128]{0,1:T(8,128)}) %all-reduce.14.cloned.1.call-update) | async-done | bytes 131088 | tf_op jit(solution)/shard_map/psum | solution.py:36
  289.2 1.9 fusion.18
  291.2 148.2 %all-reduce.16.cloned.1.call-done = f32[128,128]{0,1:T(8,128)} async-done(((f32[128,128]{0,1:T(8,128)}), f32[128,128]{0,1:T(8,128)}) %all-reduce.16.cloned.1.call-update) | async-done | bytes 65552 | tf_op jit(solution)/shard_map/psum | solution.py:37
  441.2 11.7 cholesky.59
  454.2 9.8 custom-call.10
  464.0 1.2 fusion.3
  465.2 1.3 fusion.1
  466.6 156.5 %all-reduce.18.cloned.1.call-done = bf16[2048,128]{0,1:T(8,128)(2,1)} async-done(((bf16[2048,128]{0,1:T(8,128)(2,1)}), bf16[2048,128]{0,1:T(8,128)(2,1)}) %all-reduce.18.cloned.1.call-update) | async-done | bytes 524304 | tf_op jit(solution)/shard_map/psum | solution.py:16
  623.1 3.7 convolution_bitcast_fusion
  626.8 116.4 %all-reduce.20.cloned.1.call-done = f32[896,128]{0,1:T(8,128)} async-done(((f32[896,128]{0,1:T(8,128)}), f32[896,128]{0,1:T(8,128)}) %all-reduce.20.cloned.1.call-update) | async-done | bytes 458768 | tf_op jit(solution)/shard_map/psum | solution.py:36
  743.2 2.4 fusion.19
  745.8 145.9 %all-reduce.22.cloned.1.call-done = f32[128,128]{0,1:T(8,128)} async-done(((f32[128,128]{0,1:T(8,128)}), f32[128,128]{0,1:T(8,128)}) %all-reduce.22.cloned.1.call-update) | async-done | bytes 65552 | tf_op jit(solution)/shard_map/psum | solution.py:37
  893.5 11.7 cholesky.70
  906.6 9.8 custom-call.8
  916.4 1.9 convolution_convert_fusion.4
  918.3 4.2 fusion
  922.6 156.4 %all-reduce.24.cloned.1.call-done = bf16[2048,128]{0,1:T(8,128)(2,1)} async-done(((bf16[2048,128]{0,1:T(8,128)(2,1)}), bf16[2048,128]{0,1:T(8,128)(2,1)}) %all-reduce.24.cloned.1.call-update) | async-done | bytes 524304 | tf_op jit(solution)/shard_map/psum | solution.py:16
  1079.0 2.0 convolution_bitcast_fusion.3
  1081.1 116.5 %all-reduce.26.cloned.1.call-done = f32[256,128]{0,1:T(8,128)} async-done(((f32[256,128]{0,1:T(8,128)}), f32[256,128]{0,1:T(8,128)}) %all-reduce.26.cloned.1.call-update) | async-done | bytes 131088 | tf_op jit(solution)/shard_map/psum | solution.py:36
  1197.5 1.9 fusion.20
  1199.7 147.9 %all-reduce.28.cloned.1.call-done = f32[128,128]{0,1:T(8,128)} async-done(((f32[128,128]{0,1:T(8,128)}), f32[128,128]{0,1:T(8,128)}) %all-reduce.28.cloned.1.call-update) | async-done | bytes 65552 | tf_op jit(solution)/shard_map/psum | solution.py:37
  1349.4 11.7 cholesky.81
  1362.5 9.8 custom-call.11
  1372.3 1.2 broadcast_multiply_fusion
  1373.5 1.3 fusion.2
  1374.9 156.5 %all-reduce.30.cloned.1.call-done = bf16[2048,128]{0,1:T(8,128)(2,1)} async-done(((bf16[2048,128]{0,1:T(8,128)(2,1)}), bf16[2048,128]{0,1:T(8,128)(2,1)}) %all-reduce.30.cloned.1.call-update) | async-done | bytes 524304 | tf_op jit(solution)/shard_map/psum | solution.py:16
  1531.4 3.7 fusion.21
  1535.9 115.7 %all-reduce.32.cloned.1.call-done = f32[128,896]{1,0:T(8,128)} async-done(((f32[128,896]{1,0:T(8,128)}), f32[128,896]{1,0:T(8,128)}) %all-reduce.32.cloned.1.call-update) | async-done | bytes 458768 | tf_op jit(solution)/shard_map/psum | solution.py:59
  1651.5 1.8 copy.26
  (40 shorter events, 11.2 us)
Async XLA Ops:
  7.2 163.5 %copy-start = (bf16[2048,256]{1,0:T(8,128)(2,1)S(1)}, bf16[2048,256]{1,0:T(8,128)(2,1)}, u32[]{:S(2)}) copy-start(bf16[2048,256]{1,0:T(8,128)(2,1)} %param.6) | copy-start | bytes 3145732
  7.2 163.5 %all-reduce.12.cloned.1.call-start = ((), (), s32[]{:S(2)}) async-start(), calls=%async_computation | async-start | bytes 1048576 | tf_op jit(solution)/shard_map/psum | solution.py:16
  11.3 277.9 %all-reduce.14.cloned.1.call-start = ((), (), s32[]{:S(2)}) async-start(), calls=%async_computation.1 | async-start | bytes 262144 | tf_op jit(solution)/shard_map/psum | solution.py:36
  172.8 266.6 %all-reduce.16.cloned.1.call-start = ((), (), s32[]{:S(2)}) async-start(), calls=%async_computation.2 | async-start | bytes 131072 | tf_op jit(solution)/shard_map/psum | solution.py:37
  291.1 331.9 %all-reduce.18.cloned.1.call-start = ((), (), s32[]{:S(2)}) async-start(), calls=%async_computation.3 | async-start | bytes 1048576 | tf_op jit(solution)/shard_map/psum | solution.py:16
  466.6 276.6 %all-reduce.20.cloned.1.call-start = ((), (), s32[]{:S(2)}) async-start(), calls=%async_computation.4 | async-start | bytes 917504 | tf_op jit(solution)/shard_map/psum | solution.py:36
  626.8 264.9 %all-reduce.22.cloned.1.call-start = ((), (), s32[]{:S(2)}) async-start(), calls=%async_computation.5 | async-start | bytes 131072 | tf_op jit(solution)/shard_map/psum | solution.py:37
  745.6 333.4 %all-reduce.24.cloned.1.call-start = ((), (), s32[]{:S(2)}) async-start(), calls=%async_computation.6 | async-start | bytes 1048576 | tf_op jit(solution)/shard_map/psum | solution.py:16
  922.5 275.0 %all-reduce.26.cloned.1.call-start = ((), (), s32[]{:S(2)}) async-start(), calls=%async_computation.7 | async-start | bytes 262144 | tf_op jit(solution)/shard_map/psum | solution.py:36
  1081.0 266.7 %all-reduce.28.cloned.1.call-start = ((), (), s32[]{:S(2)}) async-start(), calls=%async_computation.8 | async-start | bytes 131072 | tf_op jit(solution)/shard_map/psum | solution.py:37
  1199.4 331.9 %all-reduce.30.cloned.1.call-start = ((), (), s32[]{:S(2)}) async-start(), calls=%async_computation.9 | async-start | bytes 1048576 | tf_op jit(solution)/shard_map/psum | solution.py:16
  1374.9 276.7 %all-reduce.32.cloned.1.call-start = ((), (), s32[]{:S(2)}) async-start(), calls=%async_computation.10 | async-start | bytes 917504 | tf_op jit(solution)/shard_map/psum | solution.py:59
Sparse Core Ops, SparseCore 0:
  11.4 159.2 all-reduce.11
  173.7 115.5 all-reduce.13
  293.3 146.0 all-reduce.15
  466.7 156.3 all-reduce.17
  626.9 116.2 all-reduce.19
  747.1 144.5 all-reduce.21
  922.6 156.2 all-reduce.23
  1082.0 115.5 all-reduce.25
  1201.6 146.0 all-reduce.27
  1375.0 156.3 all-reduce.29
  1535.2 116.2 all-reduce.31
where the time goes:
time: 1660 us
  waiting for transfers between devices  1540 us (93%)
  other arithmetic  71.1 us (4%)
  matrix products  32.8 us (2%)
    psum x4, waiting for transfers between devices, token_total(): return lax.psum(partial_value.astype(jnp.bfloat16), 'mp')  629 us
    psum x3, waiting for transfers between devices, orthonormalize(): gram_matrix = lax.psum(gram_of(summed), 'mp')  442 us
    psum x3, waiting for transfers between devices, orthonormalize(): summed = lax.psum(partial_value, 'dp')  349 us
    psum x1, waiting for transfers between devices, on_device(): projection = lax.psum(projected, 'dp')  116 us
    another operation x9, other arithmetic, orthonormalize(): factor = jnp.linalg.cholesky(gram_matrix)  37.2 us
  transfers between devices with their start and end apart: 11, of which 11 were waited for; matrix products, arithmetic and copies ran while one was open for 0% of the time, Pallas kernels for 0%

commit v1 on v0

--- a/solution.py
+++ b/solution.py
@@ -34,7 +34,7 @@
 
 def orthonormalize(partial_value):
     summed = lax.psum(partial_value, "dp")
-    gram_matrix = lax.psum(gram_of(summed), "mp")
+    gram_matrix = jnp.sum(lax.all_gather(gram_of(summed), "mp"), axis=0)
     factor = jnp.linalg.cholesky(gram_matrix)
     return solve_rows(factor, summed)
 

time: 1660 us -> 1450 us (0.87)
  waiting for transfers between devices: 1540 us -> 1330 us
    psum x3 -> x0, waiting for transfers between devices: 442 us -> none  [orthonormalize(): gram_matrix = lax.psum(gram_of(summed), 'mp')]
    all_gather x0 -> x3, waiting for transfers between devices: none -> 241 us  [orthonormalize(): gram_matrix = jnp.sum(lax.all_gather(gram_of(summed), 'mp'), axis=0)]
where the time goes in v1:
time: 1450 us
  waiting for transfers between devices  1330 us (92%)
  other arithmetic  73.7 us (5%)
  matrix products  31.8 us (2%)
    psum x4, waiting for transfers between devices, token_total(): return lax.psum(partial_value.astype(jnp.bfloat16), 'mp')  624 us
    psum x3, waiting for transfers between devices, orthonormalize(): summed = lax.psum(partial_value, 'dp')  349 us
    all_gather x3, waiting for transfers between devices, orthonormalize(): gram_matrix = jnp.sum(lax.all_gather(gram_of(summed), 'mp'), axis=0)  241 us
    psum x1, waiting for transfers between devices, on_device(): projection = lax.psum(projected, 'dp')  115 us
    another operation x9, other arithmetic, orthonormalize(): factor = jnp.linalg.cholesky(gram_matrix)  37.2 us
    another operation x6, other arithmetic, solve_rows(): lax.linalg.triangular_solve(factor, matrix, left_side=False, lower=True,...  31.4 us
  transfers between devices with their start and end apart: 11, of which 11 were waited for; matrix products, arithmetic and copies ran while one was open for 0% of the time, Pallas kernels for 0%

profile of v1, /device:TPU:1, one launch (start us, length us, event | category | flops | bytes accessed | tf_op | source)
XLA Modules:
  0.0 1453.1 jit_solution(6361867439550280717)
XLA Ops:
  7.2 4.1 convolution_convert_fusion.1
  11.4 159.3 %all-reduce.9.cloned.1.call-done = bf16[2048,128]{1,0:T(8,128)(2,1)} async-done(((bf16[2048,128]{1,0:T(8,128)(2,1)}), bf16[2048,128]{1,0:T(8,128)(2,1)}) %all-reduce.9.cloned.1.call-update) | async-done | bytes 524304 | tf_op jit(solution)/shard_map/psum | solution.py:16
  170.7 2.0 convolution_bitcast_fusion.4
  172.8 116.4 %all-reduce.11.cloned.1.call-done = f32[256,128]{0,1:T(8,128)} async-done(((f32[256,128]{0,1:T(8,128)}), f32[256,128]{0,1:T(8,128)}) %all-reduce.11.cloned.1.call-update) | async-done | bytes 131088 | tf_op jit(solution)/shard_map/psum | solution.py:36
  289.2 1.9 fusion.18
  291.2 81.0 %all-gather.7.cloned.1.call-done = f32[4096,128]{1,0:T(8,128)} async-done(((f32[128,128]{1,0:T(8,128)}), f32[4096,128]{1,0:T(8,128)}) %all-gather.7.cloned.1.call-update) | async-done | bytes 2097168 | tf_op jit(solution)/shard_map/all_gather | solution.py:37
  372.2 1.7 reduce_sum.27
  374.1 11.7 cholesky.59
  387.1 9.8 custom-call.10
  398.1 1.3 fusion.1
  399.5 155.1 %all-reduce.13.cloned.1.call-done = bf16[2048,128]{0,1:T(8,128)(2,1)} async-done(((bf16[2048,128]{0,1:T(8,128)(2,1)}), bf16[2048,128]{0,1:T(8,128)(2,1)}) %all-reduce.13.cloned.1.call-update) | async-done | bytes 524304 | tf_op jit(solution)/shard_map/psum | solution.py:16
  554.6 3.7 convolution_bitcast_fusion
  558.4 116.2 %all-reduce.15.cloned.1.call-done = f32[896,128]{0,1:T(8,128)} async-done(((f32[896,128]{0,1:T(8,128)}), f32[896,128]{0,1:T(8,128)}) %all-reduce.15.cloned.1.call-update) | async-done | bytes 458768 | tf_op jit(solution)/shard_map/psum | solution.py:36
  674.6 2.5 fusion.19
  677.3 78.7 %all-gather.9.cloned.1.call-done = f32[4096,128]{1,0:T(8,128)} async-done(((f32[128,128]{1,0:T(8,128)}), f32[4096,128]{1,0:T(8,128)}) %all-gather.9.cloned.1.call-update) | async-done | bytes 2097168 | tf_op jit(solution)/shard_map/all_gather | solution.py:37
  756.0 1.7 reduce_sum.28
  757.8 11.7 cholesky.70
  770.8 9.8 custom-call.8
  781.5 4.2 fusion
  785.8 155.1 %all-reduce.17.cloned.1.call-done = bf16[2048,128]{0,1:T(8,128)(2,1)} async-done(((bf16[2048,128]{0,1:T(8,128)(2,1)}), bf16[2048,128]{0,1:T(8,128)(2,1)}) %all-reduce.17.cloned.1.call-update) | async-done | bytes 524304 | tf_op jit(solution)/shard_map/psum | solution.py:16
  940.9 2.0 convolution_bitcast_fusion.3
  943.0 116.5 %all-reduce.19.cloned.1.call-done = f32[256,128]{0,1:T(8,128)} async-done(((f32[256,128]{0,1:T(8,128)}), f32[256,128]{0,1:T(8,128)}) %all-reduce.19.cloned.1.call-update) | async-done | bytes 131088 | tf_op jit(solution)/shard_map/psum | solution.py:36
  1059.4 1.9 fusion.20
  1061.6 80.8 %all-gather.11.cloned.1.call-done = f32[4096,128]{1,0:T(8,128)} async-done(((f32[128,128]{1,0:T(8,128)}), f32[4096,128]{1,0:T(8,128)}) %all-gather.11.cloned.1.call-update) | async-done | bytes 2097168 | tf_op jit(solution)/shard_map/all_gather | solution.py:37
  1142.5 1.7 reduce_sum.29
  1144.3 11.7 cholesky.81
  1157.3 9.8 custom-call.11
  1168.4 1.3 fusion.2
  1169.7 155.0 %all-reduce.21.cloned.1.call-done = bf16[2048,128]{0,1:T(8,128)(2,1)} async-done(((bf16[2048,128]{0,1:T(8,128)(2,1)}), bf16[2048,128]{0,1:T(8,128)(2,1)}) %all-reduce.21.cloned.1.call-update) | async-done | bytes 524304 | tf_op jit(solution)/shard_map/psum | solution.py:16
  1324.7 3.7 fusion.21
  1329.2 115.5 %all-reduce.23.cloned.1.call-done = f32[128,896]{1,0:T(8,128)} async-done(((f32[128,896]{1,0:T(8,128)}), f32[128,896]{1,0:T(8,128)}) %all-reduce.23.cloned.1.call-update) | async-done | bytes 458768 | tf_op jit(solution)/shard_map/psum | solution.py:59
  1444.7 1.8 copy.21
  (45 shorter events, 9.4 us)
Async XLA Ops:
  7.2 163.5 %copy-start = (bf16[2048,256]{1,0:T(8,128)(2,1)S(1)}, bf16[2048,256]{1,0:T(8,128)(2,1)}, u32[]{:S(2)}) copy-start(bf16[2048,256]{1,0:T(8,128)(2,1)} %param.6) | copy-start | bytes 3145732
  7.2 163.5 %all-reduce.9.cloned.1.call-start = ((), (), s32[]{:S(2)}) async-start(), calls=%async_computation | async-start | bytes 1048576 | tf_op jit(solution)/shard_map/psum | solution.py:16
  11.3 277.9 %all-reduce.11.cloned.1.call-start = ((), (), s32[]{:S(2)}) async-start(), calls=%async_computation.1 | async-start | bytes 262144 | tf_op jit(solution)/shard_map/psum | solution.py:36
  172.8 199.5 %all-gather.7.cloned.1.call-start = ((), (), s32[]{:S(2)}) async-start(), calls=%async_computation.8 | async-start | bytes 2162688 | tf_op jit(solution)/shard_map/all_gather | solution.py:37
  291.1 263.4 %all-reduce.13.cloned.1.call-start = ((), (), s32[]{:S(2)}) async-start(), calls=%async_computation.2 | async-start | bytes 1048576 | tf_op jit(solution)/shard_map/psum | solution.py:16
  399.5 275.1 %all-reduce.15.cloned.1.call-start = ((), (), s32[]{:S(2)}) async-start(), calls=%async_computation.3 | async-start | bytes 917504 | tf_op jit(solution)/shard_map/psum | solution.py:36
  558.3 197.6 %all-gather.9.cloned.1.call-start = ((), (), s32[]{:S(2)}) async-start(), calls=%async_computation.9 | async-start | bytes 2162688 | tf_op jit(solution)/shard_map/all_gather | solution.py:37
  674.6 106.1 %copy-start.1 = (f32[896,128]{0,1:T(8,128)S(1)}, f32[896,128]{0,1:T(8,128)}, u32[]{:S(2)}) copy-start(f32[896,128]{0,1:T(8,128)} %all-reduce.15.cloned.1.call-done) | copy-start | bytes 1376260
  677.1 263.8 %all-reduce.17.cloned.1.call-start = ((), (), s32[]{:S(2)}) async-start(), calls=%async_computation.4 | async-start | bytes 1048576 | tf_op jit(solution)/shard_map/psum | solution.py:16
  785.8 273.7 %all-reduce.19.cloned.1.call-start = ((), (), s32[]{:S(2)}) async-start(), calls=%async_computation.5 | async-start | bytes 262144 | tf_op jit(solution)/shard_map/psum | solution.py:36
  942.9 199.5 %all-gather.11.cloned.1.call-start = ((), (), s32[]{:S(2)}) async-start(), calls=%async_computation.10 | async-start | bytes 2162688 | tf_op jit(solution)/shard_map/all_gather | solution.py:37
  1061.4 263.4 %all-reduce.21.cloned.1.call-start = ((), (), s32[]{:S(2)}) async-start(), calls=%async_computation.6 | async-start | bytes 1048576 | tf_op jit(solution)/shard_map/psum | solution.py:16
  1169.7 275.0 %all-reduce.23.cloned.1.call-start = ((), (), s32[]{:S(2)}) async-start(), calls=%async_computation.7 | async-start | bytes 917504 | tf_op jit(solution)/shard_map/psum | solution.py:59
Sparse Core Ops, SparseCore 0:
  11.4 159.2 all-reduce.8
  173.7 115.5 all-reduce.10
  293.0 79.2 all-gather.6
  399.6 154.9 all-reduce.12
  558.4 116.0 all-reduce.14
  678.2 77.7 all-gather.8
  785.9 154.9 all-reduce.16
  943.9 115.5 all-reduce.18
  1063.2 79.2 all-gather.10
  1169.8 154.9 all-reduce.20
  1328.6 116.0 all-reduce.22
